TPU v7x, 32 devices: a whole 2x2x4 slice. The times are simulated.
32 devices in a mesh: face: 4 (over x, core), tile: 8 (over z, y).
Axes of the slice: x: 2, y: 2, z: 4, core: 2. Of those that a mesh axis runs over, the one named last changes fastest.
Arguments:
- field_in: bfloat16 [12, 48, 256, 256], P('face', None, 'tile'), may hold values from -6 to 6
- out_grad: bfloat16 [12, 48, 256, 256], P('face', None, 'tile'), may hold values from -6 to 6
- weight_first: bfloat16 [48, 48, 3, 3], replicated, may hold values from -0.3125 to 0.3125
- bias_first: float32 [48], replicated, may hold values from -3 to 3
- weight_second: bfloat16 [48, 48, 3, 3], replicated, may hold values from -0.3125 to 0.3125
- bias_second: float32 [48], replicated, may hold values from -3 to 3
- face_links: int32 [12, 4, 3], replicated, may hold values from 0 to 11, as said below
- corner_rules: int32 [12, 4], replicated, may hold values from 0 to 1
Outputs:
- output_field: bfloat16 [12, 48, 256, 256], P('face', None, 'tile')
- grad_field: bfloat16 [12, 48, 256, 256], P('face', None, 'tile')
- grad_weight_first: float32 [48, 48, 3, 3], replicated
- grad_bias_first: float32 [48], replicated
- grad_weight_second: float32 [48, 48, 3, 3], replicated
- grad_bias_second: float32 [48], replicated
Inputs may be any that keep to these rules, and one draw needn't show every extreme that they name: face_links[f, e] = (g, e2, r) glues edge e of face f to edge e2 of face g; r = 1 when positions along the two edges run in opposite directions. The gluing is a pairing: (g, e2) differs from (f, e) and face_links[g, e2] = (f, e, r). The partner face lies in 0..11, the edge in 0..3, the flag in 0..1.
All inputs are finite; a program needn't handle non-finite values.
Results may differ from a plain program's by a relative error of at most 0.0055.
The roundings to bfloat16 on the way count: a program that leaves them out, or rounds other values in their place, can miss the bound.
Values may be sent and summed in bfloat16 or wider, within the bound.
A program may use at most 256 MiB of HBM per device.

v0:
```python
import jax
import jax.numpy as jnp
from jax import lax
from jax.sharding import PartitionSpec as P

INV_ROOT_TWO = 0.7071067811865476
INV_ROOT_TWO_PI = 0.3989422804014327


def shortened(x):
    return jax.tree.map(lambda a: a.astype(jnp.bfloat16) if a.dtype == jnp.float32 else a, x)


def extended_2(block, sides, width):
    for axis, dim in sides:
        count = lax.axis_size(axis)
        forward = [(i, i + 1) for i in range(count - 1)]
        backward = [(target, source) for source, target in forward]
        low = lax.ppermute(
            lax.slice_in_dim(block, block.shape[dim] - width, None, axis=dim), axis, forward
        )
        high = lax.ppermute(lax.slice_in_dim(block, 0, width, axis=dim), axis, backward)
        block = jnp.concatenate([low, block, high], axis=dim)
    return block


def gelu_pair(values):
    normal_cdf = 0.5 * (1.0 + lax.erf(values * INV_ROOT_TWO))
    normal_pdf = jnp.exp(-0.5 * values * values) * INV_ROOT_TWO_PI
    return (values * normal_cdf, normal_cdf + values * normal_pdf)


def convolve(padded, weight):
    return lax.conv_general_dilated(
        padded,
        weight,
        (1, 1),
        "VALID",
        dimension_numbers=("NCHW", "OIHW", "NCHW"),
        preferred_element_type=jnp.float32,
    )


def halo_rows(strip):
    return extended_2(shortened(strip), (("tile", 2),), 1).astype(strip.dtype)


def place_lines(north_row, south_row, west_part, east_part, tile_pos, tile_count):
    seg_len = west_part.shape[-1]
    mirrored = tile_count - 1 - tile_pos
    blanks = jnp.zeros(north_row.shape, jnp.float32)
    north_full = jnp.where(tile_pos == 0, north_row.astype(jnp.float32), blanks)
    south_full = jnp.where(tile_pos == tile_count - 1, south_row.astype(jnp.float32), blanks)
    west_wide = west_part.astype(jnp.float32)
    east_wide = east_part.astype(jnp.float32)
    west_full = lax.dynamic_update_slice_in_dim(blanks, west_wide, tile_pos * seg_len, 2)
    east_full = lax.dynamic_update_slice_in_dim(blanks, east_wide, tile_pos * seg_len, 2)
    placed = jnp.stack([north_full, south_full, west_full, east_full], axis=1)
    own_lines = lax.psum(placed.astype(jnp.bfloat16), "tile")
    front = lax.dynamic_slice_in_dim(own_lines, tile_pos * seg_len, seg_len, 3)
    back = lax.dynamic_slice_in_dim(own_lines, mirrored * seg_len, seg_len, 3)
    return (front, back)


def partner_pieces(front, my_links, tile_pos, tile_count):
    faces_dev, _, channels, seg_len = front.shape
    side_len = seg_len * tile_count
    partner_face = my_links[:, :, 0].reshape(-1)
    partner_edge = my_links[:, :, 1].reshape(-1)
    flip_mask = (my_links[:, :, 2] == 1).reshape(-1)
    gathered = lax.all_gather(front, ("face", "tile"), axis=3, tiled=True)

    def fetch_line(face_id, edge_id):
        start = (face_id % faces_dev, edge_id, 0, face_id // faces_dev * side_len)
        return lax.dynamic_slice(gathered, start, (1, 1, channels, side_len))[0, 0]

    source = jax.vmap(fetch_line)(partner_face, partner_edge)
    ghosts = jnp.where(flip_mask[:, None, None], source[:, :, ::-1], source)
    ghosts = ghosts.reshape(faces_dev, 4, channels, side_len)
    north_row = ghosts[:, 0]
    south_row = ghosts[:, 1]
    west_part = lax.dynamic_slice_in_dim(ghosts[:, 2], tile_pos * seg_len, seg_len, 2)
    east_part = lax.dynamic_slice_in_dim(ghosts[:, 3], tile_pos * seg_len, seg_len, 2)
    return (north_row, south_row, west_part, east_part)


def fill_strip(activation, my_links, my_corners, tile_pos, tile_count):
    front, back = place_lines(
        activation[:, :, 0, :],
        activation[:, :, -1, :],
        activation[:, :, :, 0],
        activation[:, :, :, -1],
        tile_pos,
        tile_count,
    )
    north_row, south_row, west_part, east_part = partner_pieces(
        front, my_links, tile_pos, tile_count
    )
    corner_code = (my_corners == 0)[:, :, None]
    corner_nw = jnp.where(corner_code[:, 0], north_row[:, :, 0], west_part[:, :, 0])
    corner_ne = jnp.where(corner_code[:, 1], north_row[:, :, -1], east_part[:, :, 0])
    corner_sw = jnp.where(corner_code[:, 2], south_row[:, :, 0], west_part[:, :, -1])
    corner_se = jnp.where(corner_code[:, 3], south_row[:, :, -1], east_part[:, :, -1])
    middle = jnp.concatenate(
        [west_part[:, :, :, None], activation, east_part[:, :, :, None]], axis=3
    )
    extended = halo_rows(middle)
    top_row = jnp.concatenate([corner_nw[:, :, None], north_row, corner_ne[:, :, None]], axis=2)
    bottom_row = jnp.concatenate([corner_sw[:, :, None], south_row, corner_se[:, :, None]], axis=2)
    top_rim = jnp.where(tile_pos == 0, top_row, extended[:, :, 0])
    bottom_rim = jnp.where(tile_pos == tile_count - 1, bottom_row, extended[:, :, -1])
    return jnp.concatenate(
        [top_rim[:, :, None], extended[:, :, 1:-1], bottom_rim[:, :, None]], axis=2
    )


def unfold_strip(cotangent, weight, my_links, my_corners, tile_pos, tile_count):
    widened = jnp.pad(cotangent, ((0, 0), (0, 0), (0, 0), (1, 1)))
    extended = halo_rows(widened)
    padded = jnp.pad(extended, ((0, 0), (0, 0), (1, 1), (1, 1)))
    flipped = jnp.transpose(weight[:, :, ::-1, ::-1], (1, 0, 2, 3))
    pad_grad = convolve(padded, flipped)
    at_top = tile_pos == 0
    at_bottom = tile_pos == tile_count - 1
    north_row = pad_grad[:, :, 0, 1:-1]
    south_row = pad_grad[:, :, -1, 1:-1]
    west_part = pad_grad[:, :, 1:-1, 0]
    east_part = pad_grad[:, :, 1:-1, -1]
    corner_nw = pad_grad[:, :, 0, 0]
    corner_ne = pad_grad[:, :, 0, -1]
    corner_sw = pad_grad[:, :, -1, 0]
    corner_se = pad_grad[:, :, -1, -1]
    corner_code = my_corners[:, :, None]
    north_row = north_row.at[:, :, 0].add(jnp.where(corner_code[:, 0] == 0, corner_nw, 0.0))
    north_row = north_row.at[:, :, -1].add(jnp.where(corner_code[:, 1] == 0, corner_ne, 0.0))
    south_row = south_row.at[:, :, 0].add(jnp.where(corner_code[:, 2] == 0, corner_sw, 0.0))
    south_row = south_row.at[:, :, -1].add(jnp.where(corner_code[:, 3] == 0, corner_se, 0.0))
    west_part = west_part.at[:, :, 0].add(
        jnp.where((corner_code[:, 0] == 1) & at_top, corner_nw, 0.0)
    )
    west_part = west_part.at[:, :, -1].add(
        jnp.where((corner_code[:, 2] == 1) & at_bottom, corner_sw, 0.0)
    )
    east_part = east_part.at[:, :, 0].add(
        jnp.where((corner_code[:, 1] == 1) & at_top, corner_ne, 0.0)
    )
    east_part = east_part.at[:, :, -1].add(
        jnp.where((corner_code[:, 3] == 1) & at_bottom, corner_se, 0.0)
    )
    front, back = place_lines(
        north_row.astype(jnp.bfloat16),
        south_row.astype(jnp.bfloat16),
        west_part.astype(jnp.bfloat16),
        east_part.astype(jnp.bfloat16),
        tile_pos,
        tile_count,
    )
    back_north, back_south, back_west, back_east = partner_pieces(
        front, my_links, tile_pos, tile_count
    )
    interior = pad_grad[:, :, 1:-1, 1:-1]
    interior = interior.at[:, :, 0, :].add(jnp.where(at_top, back_north.astype(jnp.float32), 0.0))
    interior = interior.at[:, :, -1, :].add(
        jnp.where(at_bottom, back_south.astype(jnp.float32), 0.0)
    )
    interior = interior.at[:, :, :, 0].add(back_west.astype(jnp.float32))
    interior = interior.at[:, :, :, -1].add(back_east.astype(jnp.float32))
    return interior


def weight_grad(cotangent, padded):
    return lax.conv_general_dilated(
        padded,
        cotangent,
        (1, 1),
        "VALID",
        dimension_numbers=("CNHW", "IOHW", "CNHW"),
        preferred_element_type=jnp.float32,
    )


def body(
    field_in,
    out_grad,
    weight_first,
    bias_first,
    weight_second,
    bias_second,
    face_links,
    corner_rules,
):
    tile_count = lax.axis_size("tile")
    tile_pos = lax.axis_index("tile")
    face_pos = lax.axis_index("face")
    faces_dev = field_in.shape[0]
    side_len = field_in.shape[3]
    my_links = lax.dynamic_slice_in_dim(face_links, face_pos * faces_dev, faces_dev, 0)
    my_corners = lax.dynamic_slice_in_dim(corner_rules, face_pos * faces_dev, faces_dev, 0)
    padded_first = fill_strip(field_in, my_links, my_corners, tile_pos, tile_count)
    pre_first = convolve(padded_first, weight_first) + bias_first[None, :, None, None]
    gelu_first, slope_first = gelu_pair(pre_first)
    hidden = gelu_first.astype(jnp.bfloat16)
    padded_second = fill_strip(hidden, my_links, my_corners, tile_pos, tile_count)
    pre_second = convolve(padded_second, weight_second) + bias_second[None, :, None, None]
    gelu_second, slope_second = gelu_pair(pre_second)
    output_field = gelu_second.astype(jnp.bfloat16)
    grad_second = (out_grad.astype(jnp.float32) * slope_second).astype(jnp.bfloat16)
    weight_second_part = weight_grad(grad_second, padded_second)
    bias_second_part = jnp.sum(grad_second.astype(jnp.float32), axis=(0, 2, 3))
    grad_hidden = unfold_strip(
        grad_second, weight_second, my_links, my_corners, tile_pos, tile_count
    )
    grad_first = (grad_hidden * slope_first).astype(jnp.bfloat16)
    weight_first_part = weight_grad(grad_first, padded_first)
    bias_first_part = jnp.sum(grad_first.astype(jnp.float32), axis=(0, 2, 3))
    grad_field = unfold_strip(
        grad_first, weight_first, my_links, my_corners, tile_pos, tile_count
    ).astype(jnp.bfloat16)
    totals = lax.psum(
        (weight_first_part, bias_first_part, weight_second_part, bias_second_part), ("face", "tile")
    )
    return (
        output_field,
        grad_field,
        totals[0] / side_len,
        totals[1] / side_len,
        totals[2] / side_len,
        totals[3] / side_len,
    )


def solution(mesh):
    return jax.shard_map(
        body,
        mesh=mesh,
        in_specs=(
            P("face", None, "tile", None),
            P("face", None, "tile", None),
            P(),
            P(),
            P(),
            P(),
            P(),
            P(),
        ),
        out_specs=(
            P("face", None, "tile", None),
            P("face", None, "tile", None),
            P(),
            P(),
            P(),
            P(),
        ),
        check_vma=False,
    )
```

profile of v0, /device:TPU:0, one launch (start us, length us, event | category | flops | bytes accessed | tf_op | source)
XLA Modules:
  0.0 1963.4 jit_solution(1567796698921269111)
XLA Ops:
  19.2 74.5 %all-reduce.10.cloned.1.call-done = bf16[3,4,48,256]{3,2,0,1:T(8,128)(2,1)} async-done(((bf16[3,4,48,256]{3,2,0,1:T(8,128)(2,1)}), bf16[3,4,48,256]{3,2,0,1:T(8,128)(2,1)}) %all-reduce.10.cloned.1.call-update) | async-done | bytes 294928 | tf_op jit(solution)/shard_map/psum | solution.py:59
  103.9 51.9 %all-gather.5.cloned.1.call-done = bf16[3,4,48,1024]{2,1,0,3:T(4,128)(2,1)} async-done(((bf16[3,4,48,32]{2,1,0,3:T(4,128)(2,1)}), bf16[3,4,48,1024]{2,1,0,3:T(4,128)(2,1)}) %all-gather.5.cloned.1.call-update) | async-done | bytes 1179664 | tf_op jit(solution)/shard_map/all_gather | solution.py:71
  179.5 17.8 fusion.87
  203.9 24.2 %copy.2867 = bf16[48,34,3,8,33]{4,3,0,2,1:T(8,128)(2,1)} copy(bf16[48,34,3,8,33]{0,2,4,3,1:T(4,128)(2,1)} %bitcast.324) | data formatting | bytes 5170176 | tf_op jit(solution)/shard_map/conv_general_dilated | solution.py:34
  268.8 23.4 %fusion.8 = (f32[32,24,33,48]{3,1,2,0:T(8,128)}, bf16[32,24,33,48]{3,1,2,0:T(8,128)(2,1)S(1)}) fusion(f32[48]{0:T(128)S(1)} %copy-done.49, pred[24,33]{0,1:T(8,128)(4,1)S(1)} %copy-done.53, bf16[48,48,3,3]{1,0,3,2:T(8,128)(2,1)S(1)} %copy-done.47, bf16[48,34,3,8,35]{0,3,2,4,1:T(8,128)(2,1)} %copy.2762), kind=kOutput, calls=%fused_computation.21 | convolution fusion | flops 1065664512 | bytes 10083288 | tf_op jit(solution)/shard_map/conv_general_dilated | solution.py:34
  311.7 72.1 %all-reduce.12.cloned.1.call-done = bf16[3,4,48,256]{3,2,0,1:T(8,128)(2,1)} async-done(((bf16[3,4,48,256]{3,2,0,1:T(8,128)(2,1)}), bf16[3,4,48,256]{3,2,0,1:T(8,128)(2,1)}) %all-reduce.12.cloned.1.call-update) | async-done | bytes 294928 | tf_op jit(solution)/shard_map/psum | solution.py:59
  386.0 59.4 %all-gather.7.cloned.1.call-done = bf16[3,4,48,1024]{2,1,0,3:T(4,128)(2,1)} async-done(((bf16[3,4,48,32]{2,1,0,3:T(4,128)(2,1)}), bf16[3,4,48,1024]{2,1,0,3:T(4,128)(2,1)}) %all-gather.7.cloned.1.call-update) | async-done | bytes 1179664 | tf_op jit(solution)/shard_map/all_gather | solution.py:71
  468.6 19.1 fusion.84
  494.3 24.2 %copy.2872 = bf16[48,34,3,8,33]{4,3,0,2,1:T(8,128)(2,1)} copy(bf16[48,34,3,8,33]{0,2,4,3,1:T(4,128)(2,1)} %bitcast.325) | data formatting | bytes 5170176 | tf_op jit(solution)/shard_map/conv_general_dilated | solution.py:34
  559.2 22.5 %fusion.12 = (f32[32,24,33,48]{3,1,2,0:T(8,128)}, bf16[32,24,33,48]{3,1,2,0:T(8,128)(2,1)}) fusion(f32[48]{0:T(128)S(1)} %copy-done.50, pred[24,33]{0,1:T(8,128)(4,1)S(1)} %copy-done.53, bf16[48,48,3,3]{1,0,3,2:T(8,128)(2,1)S(1)} %copy-done, bf16[48,34,3,8,35]{0,3,2,4,1:T(8,128)(2,1)} %copy.2782), kind=kOutput, calls=%fused_computation.25 | convolution fusion | flops 1065664512 | bytes 10083288 | tf_op jit(solution)/shard_map/conv_general_dilated | solution.py:34
  694.7 22.0 %convolution_select_fusion.1 = f32[34,24,33,48]{3,1,2,0:T(8,128)} fusion(bf16[48,48,3,3]{1,0,3,2:T(8,128)(2,1)S(1)} %copy-done, bf16[48,34,3,8,35]{0,3,2,4,1:T(8,128)(2,1)} %copy.2790, pred[24,33]{0,1:T(8,128)(4,1)S(1)} %copy-done.51), kind=kOutput, calls=%fused_computation.37 | convolution fusion | flops 1096153344 | bytes 7954200 | tf_op jit(solution)/shard_map/conv_general_dilated | solution.py:34
  746.0 17.6 copy.2888
  763.6 29.2 %fusion.67 = (f32[3,48,1,256]{2,1,0,3:T(8,128)}, f32[3,48,1,256]{2,1,0,3:T(8,128)}) fusion(f32[3,48,34,258]{2,1,0,3:T(8,128)} %bitcast.309), kind=kLoop, calls=%fused_computation.219 | loop fusion | bytes 589824 | tf_op jit(solution)/shard_map/slice | solution.py:125
  827.4 73.5 %all-reduce.14.cloned.1.call-done = bf16[3,4,48,256]{3,2,0,1:T(8,128)(2,1)} async-done(((bf16[3,4,48,256]{3,2,0,1:T(8,128)(2,1)}), bf16[3,4,48,256]{3,2,0,1:T(8,128)(2,1)}) %all-reduce.14.cloned.1.call-update) | async-done | bytes 294928 | tf_op jit(solution)/shard_map/psum | solution.py:59
  982.4 20.5 %slice_add_fusion.3 = f32[3,48,1,256]{2,1,0,3:T(8,128)} fusion(f32[3,48,1,256]{2,1,0,3:T(8,128)} %copy.2815, f32[3,48,34,258]{2,1,0,3:T(8,128)} %bitcast.315), kind=kLoop, calls=%fused_computation.14 | loop fusion | flops 36864 | bytes 442368 | tf_op jit(solution)/shard_map/add | solution.py:162
  1015.1 43.6 %scatter-add.94 = f32[3,48,32,256]{2,1,0,3:T(8,128)} dynamic-update-slice(f32[3,48,32,256]{2,1,0,3:T(8,128)} %slice.1002, f32[3,48,1,256]{2,1,0,3:T(8,128)} %slice_add_fusion.3, s32[]{:T(128)} %constant.616.clone.1, s32[]{:T(128)} %constant.616.clone.1, s32[]{:T(128)} %constant.616.clone.1, s32[]{:T(128)} %constant.616.clone.1) | dynamic-update-slice | bytes 294916 | tf_op jit(solution)/shard_map/scatter-add | solution.py:162
  1058.7 20.5 %slice_add_fusion.2 = f32[3,48,1,256]{2,1,0,3:T(8,128)} fusion(f32[3,48,1,256]{2,1,0,3:T(8,128)} %copy.2817, f32[3,48,32,256]{2,1,0,3:T(8,128)} %scatter-add.94), kind=kLoop, calls=%fused_computation.13 | loop fusion | flops 36864 | bytes 442368 | tf_op jit(solution)/shard_map/add | solution.py:163
  1079.2 73.5 %scatter-add.95 = f32[3,48,32,256]{2,1,0,3:T(8,128)} dynamic-update-slice(f32[3,48,32,256]{2,1,0,3:T(8,128)} %scatter-add.94, f32[3,48,1,256]{2,1,0,3:T(8,128)} %slice_add_fusion.2, s32[]{:T(128)} %constant.616.clone.1, s32[]{:T(128)} %constant.616.clone.1, s32[]{:T(128)} %constant.635.clone.1, s32[]{:T(128)} %constant.616.clone.1) | dynamic-update-slice | bytes 294916 | tf_op jit(solution)/shard_map/scatter-add | solution.py:163
  1207.4 44.8 %fusion.75 = f32[48,48,3,3]{0,1,3,2:T(8,128)} fusion(bf16[3,48,32,256]{1,0,3,2:T(4,128)(2,1)} %copy.2858, bf16[3,48,1,258]{1,0,3,2:T(4,128)(2,1)S(1)} %copy-done.15, bf16[3,48,32,1]{1,0,3,2:T(4,128)(2,1)S(1)} %copy-done.23, bf16[3,48,32,256]{1,0,3,2:T(4,128)(2,1)} %bitcast.319, bf16[3,48,32,1]{1,0,3,2:T(4,128)(2,1)S(1)} %copy-done.21, ...), kind=kOutput, calls=%fused_computation.227 | convolution fusion | flops 1031847552 | bytes 4968576 | tf_op jit(solution)/shard_map/conv_general_dilated | solution.py:172
  1342.3 21.8 %convolution_select_fusion = f32[34,24,33,48]{3,1,2,0:T(8,128)} fusion(bf16[48,48,3,3]{1,0,3,2:T(8,128)(2,1)S(1)} %copy-done.48, bf16[48,34,3,8,35]{0,3,2,4,1:T(8,128)(2,1)} %copy.2828, pred[24,33]{0,1:T(8,128)(4,1)S(1)} %copy-done.52), kind=kOutput, calls=%fused_computation.36 | convolution fusion | flops 1096153344 | bytes 7954200 | tf_op jit(solution)/shard_map/conv_general_dilated | solution.py:34
  1393.4 17.6 copy.2892
  1411.0 29.3 %fusion.66 = (f32[3,48,1,256]{2,1,0,3:T(8,128)}, f32[3,48,1,256]{2,1,0,3:T(8,128)}) fusion(f32[3,48,34,258]{2,1,0,3:T(8,128)} %bitcast.302), kind=kLoop, calls=%fused_computation.218 | loop fusion | bytes 589824 | tf_op jit(solution)/shard_map/slice | solution.py:125
  1475.0 44.8 %fusion.74 = f32[48,48,3,3]{0,1,3,2:T(8,128)} fusion(bf16[3,48,32,256]{1,0,3,2:T(4,128)(2,1)} %copy.2857, bf16[3,48,1,258]{1,0,3,2:T(4,128)(2,1)S(1)} %copy-done.11, bf16[3,48,32,1]{1,0,3,2:T(4,128)(2,1)S(1)} %copy-done.19, bf16[3,48,32,256]{1,0,3,2:T(4,128)(2,1)} %copy.2758, bf16[3,48,32,1]{1,0,3,2:T(4,128)(2,1)S(1)} %copy-done.17, ...), kind=kOutput, calls=%fused_computation.226 | convolution fusion | flops 1031847552 | bytes 4968576 | tf_op jit(solution)/shard_map/conv_general_dilated | solution.py:172
  1520.1 28.0 %all-reduce.16.cloned.1.call-done = bf16[3,4,48,256]{3,2,0,1:T(8,128)(2,1)} async-done(((bf16[3,4,48,256]{3,2,0,1:T(8,128)(2,1)}), bf16[3,4,48,256]{3,2,0,1:T(8,128)(2,1)}) %all-reduce.16.cloned.1.call-update) | async-done | bytes 294928 | tf_op jit(solution)/shard_map/psum | solution.py:59
  1567.8 39.3 %all-reduce.2 = (f32[48]{0:T(128)S(1)}, f32[48]{0:T(128)S(1)}) all-reduce(f32[48]{0:T(128)S(1)} %copy-done.46, f32[48]{0:T(128)S(1)} %copy-done.45), channel_id=1, replica_groups=mesh['face'=4,'tile'=8] {'face','tile'}, use_global_device_ids=true, to_apply=%region_6.7 | all-reduce | flops 96 | bytes 768 | tf_op jit(solution)/shard_map/psum | solution.py:219
  1608.2 16.6 slice.1030
  1624.8 54.6 %all-reduce.18.cloned.1.call-done = (f32[48,48,3,3]{0,1,3,2:T(8,128)}, f32[48,48,3,3]{0,1,3,2:T(8,128)}) async-done(((f32[48,48,3,3]{0,1,3,2:T(8,128)}, f32[48,48,3,3]{0,1,3,2:T(8,128)}), (f32[48,48,3,3]{0,1,3,2:T(8,128)}, f32[48,48,3,3]{0,1,3,2:T(8,128)})) %all-reduce.18.cloned.1.call-update) | async-done | bytes 165904 | tf_op jit(solution)/shard_map/psum | solution.py:219
  1683.0 60.5 %all-gather.11.cloned.1.call-done = bf16[3,4,48,1024]{2,1,0,3:T(4,128)(2,1)} async-done(((bf16[3,4,48,32]{2,1,0,3:T(4,128)(2,1)}), bf16[3,4,48,1024]{2,1,0,3:T(4,128)(2,1)}) %all-gather.11.cloned.1.call-update) | async-done | bytes 1179664 | tf_op jit(solution)/shard_map/all_gather | solution.py:71
  1760.5 20.5 %slice_add_fusion.1 = f32[3,48,1,256]{2,1,0,3:T(8,128)} fusion(f32[3,48,1,256]{2,1,0,3:T(8,128)} %copy.2852, f32[3,48,34,258]{2,1,0,3:T(8,128)} %bitcast.308), kind=kLoop, calls=%fused_computation.12 | loop fusion | flops 36864 | bytes 442368 | tf_op jit(solution)/shard_map/add | solution.py:162
  1793.2 43.6 %scatter-add.114 = f32[3,48,32,256]{2,1,0,3:T(8,128)} dynamic-update-slice(f32[3,48,32,256]{2,1,0,3:T(8,128)} %slice.1030, f32[3,48,1,256]{2,1,0,3:T(8,128)} %slice_add_fusion.1, s32[]{:T(128)} %constant.616.clone.1, s32[]{:T(128)} %constant.616.clone.1, s32[]{:T(128)} %constant.616.clone.1, s32[]{:T(128)} %constant.616.clone.1) | dynamic-update-slice | bytes 294916 | tf_op jit(solution)/shard_map/scatter-add | solution.py:162
  1836.8 20.5 %slice_add_fusion = f32[3,48,1,256]{2,1,0,3:T(8,128)} fusion(f32[3,48,1,256]{2,1,0,3:T(8,128)} %copy.2854, f32[3,48,32,256]{2,1,0,3:T(8,128)} %scatter-add.114), kind=kLoop, calls=%fused_computation.11 | loop fusion | flops 36864 | bytes 442368 | tf_op jit(solution)/shard_map/add | solution.py:163
  1857.3 73.6 %scatter-add.115 = f32[3,48,32,256]{2,1,0,3:T(8,128)} dynamic-update-slice(f32[3,48,32,256]{2,1,0,3:T(8,128)} %scatter-add.114, f32[3,48,1,256]{2,1,0,3:T(8,128)} %slice_add_fusion, s32[]{:T(128)} %constant.616.clone.1, s32[]{:T(128)} %constant.616.clone.1, s32[]{:T(128)} %constant.635.clone.1, s32[]{:T(128)} %constant.616.clone.1) | dynamic-update-slice | bytes 294916 | tf_op jit(solution)/shard_map/scatter-add | solution.py:163
  (365 shorter events, 742.7 us)
Async XLA Ops:
  7.2 552.0 %copy-start = (bf16[48,48,3,3]{1,0,3,2:T(8,128)(2,1)S(1)}, bf16[48,48,3,3]{1,0,3,2:T(8,128)(2,1)}, u32[]{:S(2)}) copy-start(bf16[48,48,3,3]{1,0,3,2:T(8,128)(2,1)} %param.60) | copy-start | bytes 124420
  7.2 86.5 %all-reduce.10.cloned.1.call-start = ((), (), s32[]{:S(2)}) async-start(), calls=%async_computation | async-start | bytes 589824 | tf_op jit(solution)/shard_map/psum | solution.py:59
  7.2 95.1 %copy-start.24 = (s32[12,4,3]{0,1,2:T(4,128)S(1)}, s32[12,4,3]{0,1,2:T(4,128)}, u32[]{:S(2)}) copy-start(s32[12,4,3]{0,1,2:T(4,128)} %param.62) | copy-start | bytes 1732
  7.3 96.2 %copy-start.44 = (s32[12,4]{0,1:T(4,128)S(1)}, s32[12,4]{0,1:T(4,128)}, u32[]{:S(2)}) copy-start(s32[12,4]{0,1:T(4,128)} %param.63) | copy-start | bytes 580
  19.2 136.6 %all-gather.5.cloned.1.call-start = ((), (), s32[]{:S(2)}) async-start(), calls=%async_computation.1 | async-start | bytes 3244032 | tf_op jit(solution)/shard_map/all_gather | solution.py:71
  95.5 288.3 %all-reduce.12.cloned.1.call-start = ((), (), s32[]{:S(2)}) async-start(), calls=%async_computation.2 | async-start | bytes 589824 | tf_op jit(solution)/shard_map/psum | solution.py:59
  103.4 345.7 %copy-start.25 = (pred[12]{0:T(512)(128)(4,1)}, pred[12]{0:T(512)(128)(4,1)S(1)}, u32[]{:S(2)}) copy-start(pred[12]{0:T(512)(128)(4,1)S(1)} %eq.133) | copy-start | bytes 40
  103.9 341.5 %copy-start.5 = (s32[12]{0:T(128)}, s32[12]{0:T(128)S(1)}, u32[]{:S(2)}) copy-start(s32[12]{0:T(128)S(1)} %fusion.63) | copy-start | bytes 148
  163.5 15.4 collective-permute-start
  167.1 12.0 collective-permute-start.1
  311.7 133.7 %all-gather.7.cloned.1.call-start = ((), (), s32[]{:S(2)}) async-start(), calls=%async_computation.3 | async-start | bytes 3244032 | tf_op jit(solution)/shard_map/all_gather | solution.py:71
  385.6 515.3 %all-reduce.14.cloned.1.call-start = ((), (), s32[]{:S(2)}) async-start(), calls=%async_computation.4 | async-start | bytes 589824 | tf_op jit(solution)/shard_map/psum | solution.py:59
  452.9 15.1 collective-permute-start.2
  456.3 12.0 collective-permute-start.3
  621.4 13.5 collective-permute-start.4
  625.8 9.1 collective-permute-start.5
  627.4 192.8 %copy-start.38 = (pred[3]{0:T(512)(128)(4,1)}, pred[3]{0:T(512)(128)(4,1)S(1)}, u32[]{:S(2)}) copy-start(pred[3]{0:T(512)(128)(4,1)S(1)} %get-tuple-element.458) | copy-start | bytes 13
  627.4 192.8 %copy-start.40 = (pred[3]{0:T(512)(128)(4,1)}, pred[3]{0:T(512)(128)(4,1)S(1)}, u32[]{:S(2)}) copy-start(pred[3]{0:T(512)(128)(4,1)S(1)} %get-tuple-element.462) | copy-start | bytes 13
  627.4 192.8 %copy-start.42 = (pred[3]{0:T(512)(128)(4,1)}, pred[3]{0:T(512)(128)(4,1)S(1)}, u32[]{:S(2)}) copy-start(pred[3]{0:T(512)(128)(4,1)S(1)} %get-tuple-element.463) | copy-start | bytes 13
  627.5 194.5 %copy-start.30 = (pred[3]{0:T(512)(128)(4,1)}, pred[3]{0:T(512)(128)(4,1)S(1)}, u32[]{:S(2)}) copy-start(pred[3]{0:T(512)(128)(4,1)S(1)} %get-tuple-element.456) | copy-start | bytes 13
  627.5 194.5 %copy-start.32 = (pred[3]{0:T(512)(128)(4,1)}, pred[3]{0:T(512)(128)(4,1)S(1)}, u32[]{:S(2)}) copy-start(pred[3]{0:T(512)(128)(4,1)S(1)} %get-tuple-element.457) | copy-start | bytes 13
  627.5 194.5 %copy-start.34 = (pred[3]{0:T(512)(128)(4,1)}, pred[3]{0:T(512)(128)(4,1)S(1)}, u32[]{:S(2)}) copy-start(pred[3]{0:T(512)(128)(4,1)S(1)} %get-tuple-element.460) | copy-start | bytes 13
  627.5 194.5 %copy-start.36 = (pred[3]{0:T(512)(128)(4,1)}, pred[3]{0:T(512)(128)(4,1)S(1)}, u32[]{:S(2)}) copy-start(pred[3]{0:T(512)(128)(4,1)S(1)} %get-tuple-element.461) | copy-start | bytes 13
  627.5 196.7 %copy-start.28 = (pred[3]{0:T(512)(128)(4,1)}, pred[3]{0:T(512)(128)(4,1)S(1)}, u32[]{:S(2)}) copy-start(pred[3]{0:T(512)(128)(4,1)S(1)} %get-tuple-element.459) | copy-start | bytes 13
  827.4 137.6 %all-gather.9.cloned.1.call-start = ((), (), s32[]{:S(2)}) async-start(), calls=%async_computation.5 | async-start | bytes 3244032 | tf_op jit(solution)/shard_map/all_gather | solution.py:71
  902.8 645.3 %all-reduce.16.cloned.1.call-start = ((), (), s32[]{:S(2)}) async-start(), calls=%async_computation.6 | async-start | bytes 589824 | tf_op jit(solution)/shard_map/psum | solution.py:59
  1191.2 90.2 %collective-permute-start.6 = (bf16[3,48,1,258]{3,1,2,0:T(8,128)(2,1)}, bf16[3,48,1,258]{3,1,2,0:T(8,128)(2,1)}, u32[]{:S(2)}, u32[]{:S(2)}) collective-permute-start(bf16[3,48,1,258]{3,1,2,0:T(8,128)(2,1)} %copy.2824), channel_id=1, source_target_pairs={{0,1},{1,2},{2,3},{3,4},{4,5},{5,6},{6,7},{8,9},{9,10},{10,11},{11... | collective-permute-start | bytes 222920 | tf_op jit(solution)/shard_map/ppermute | solution.py:19
  1206.1 75.3 %collective-permute-start.7 = (bf16[3,48,1,258]{3,1,2,0:T(8,128)(2,1)}, bf16[3,48,1,258]{3,1,2,0:T(8,128)(2,1)}, u32[]{:S(2)}, u32[]{:S(2)}) collective-permute-start(bf16[3,48,1,258]{3,1,2,0:T(8,128)(2,1)} %copy.2825), channel_id=1, source_target_pairs={{1,0},{2,1},{3,2},{4,3},{5,4},{6,5},{7,6},{9,8},{10,9},{11,10},{12... | collective-permute-start | bytes 222920 | tf_op jit(solution)/shard_map/ppermute | solution.py:22
  1474.9 204.5 %all-reduce.18.cloned.1.call-start = ((), (), s32[]{:S(2)}) async-start(), calls=%async_computation.8 | async-start | bytes 884736 | tf_op jit(solution)/shard_map/psum | solution.py:219
  1519.8 223.6 %all-gather.11.cloned.1.call-start = ((), (), s32[]{:S(2)}) async-start(), calls=%async_computation.7 | async-start | bytes 3244032 | tf_op jit(solution)/shard_map/all_gather | solution.py:71
  1608.2 135.2 %copy-start.7 = (s32[12]{0:T(128)S(1)}, s32[12]{0:T(128)}, u32[]{:S(2)}) copy-start(s32[12]{0:T(128)} %copy-done.5) | copy-start | bytes 148
  1608.2 139.0 %copy-start.27 = (pred[12]{0:T(512)(128)(4,1)S(1)}, pred[12]{0:T(512)(128)(4,1)}, u32[]{:S(2)}) copy-start(pred[12]{0:T(512)(128)(4,1)} %copy-done.25) | copy-start | bytes 40
  (39 other events, 895.6 us)
Sparse Core Ops, SparseCore 0:
  19.3 74.3 all-reduce.9
  97.6 58.1 all-gather.4
  311.8 71.9 all-reduce.11
  387.2 58.1 all-gather.6
  827.5 73.4 all-reduce.13
  904.7 58.1 all-gather.8
  1475.0 72.9 all-reduce.15
  1554.0 125.3 all-reduce.17
  1683.3 60.0 all-gather.10
where the time goes:
time: 1990 us; the launch traced here: 1960 us
  local copies, waits for them, and re-layouts  973 us (49%)
  waiting for transfers between devices  499 us (25%)
  other arithmetic  236 us (12%)
  matrix products  179 us (9%)
  blocking collectives  39.3 us (2%)
  starting transfers between devices  21.1 us (1%)
    psum x4, waiting for transfers between devices, place_lines(): own_lines = lax.psum(placed.astype(jnp.bfloat16), 'tile')  248 us
    conv_general_dilated x16, local copies, waits for them, and re-layouts, convolve(): lax.conv_general_dilated(padded, weight, (1, 1), 'VALID', dimension_numbe...  238 us
    all_gather x4, waiting for transfers between devices, partner_pieces(): gathered = lax.all_gather(front, ('face', 'tile'), axis=3, tiled=True)  172 us
    scatter-add x2, local copies, waits for them, and re-layouts, unfold_strip(): interior.at[:, :, -1, :]  147 us
    unnamed x128, local copies, waits for them, and re-layouts  125 us
    conv_general_dilated x4, matrix products, convolve(): lax.conv_general_dilated(padded, weight, (1, 1), 'VALID', dimension_numbe...  89.7 us
    conv_general_dilated x2, matrix products, weight_grad(): lax.conv_general_dilated(padded, cotangent, (1, 1), 'VALID', dimension_nu...  89.7 us
    scatter-add x2, local copies, waits for them, and re-layouts, unfold_strip(): interior.at[:, :, 0, :]  87.2 us
  transfers between devices with their start and end apart: 17, of which 11 were waited for; matrix products, arithmetic and copies ran while one was open for 13% of the time, Pallas kernels for 0%

commit v1 on v0

--- a/solution.py
+++ b/solution.py
@@ -56,7 +56,7 @@
     west_full = lax.dynamic_update_slice_in_dim(blanks, west_wide, tile_pos * seg_len, 2)
     east_full = lax.dynamic_update_slice_in_dim(blanks, east_wide, tile_pos * seg_len, 2)
     placed = jnp.stack([north_full, south_full, west_full, east_full], axis=1)
-    own_lines = lax.psum(placed.astype(jnp.bfloat16), "tile")
+    own_lines = lax.all_gather(placed.astype(jnp.bfloat16), "tile").sum(axis=0)
     front = lax.dynamic_slice_in_dim(own_lines, tile_pos * seg_len, seg_len, 3)
     back = lax.dynamic_slice_in_dim(own_lines, mirrored * seg_len, seg_len, 3)
     return (front, back)

time: 1990 us -> 1360 us (0.68)
  local copies, waits for them, and re-layouts: 973 us -> 497 us
  waiting for transfers between devices: 499 us -> 421 us
  other arithmetic: 236 us -> 165 us
    psum x4 -> x0, waiting for transfers between devices: 248 us -> none  [place_lines(): own_lines = lax.psum(placed.astype(jnp.bfloat16), 'tile')]
    all_gather x0 -> x4, waiting for transfers between devices: none -> 169 us  [place_lines(): own_lines = lax.all_gather(placed.astype(jnp.bfloat16), 'tile').sum(axis=0)]
    scatter-add x2 -> x4, local copies, waits for them, and re-layouts: 147 us -> 11.3 us  [the longest x2 5.64 us: unfold_strip(): interior = interior.at[:, :, :, -1].add(back_east.astype(jnp.float32))]
    scatter-add x2 -> x1, local copies, waits for them, and re-layouts: 87.2 us -> 0.77 us  [unfold_strip(): interior.at[:, :, 0, :]]
    slice x4 -> x1, local copies, waits for them, and re-layouts: 84.9 us -> 0.54 us  [unfold_strip(): north_row = pad_grad[:, :, 0, 1:-1]]
    select_n x4 -> x0, local copies, waits for them, and re-layouts: 48.8 us -> none  [the longest x2 24.4 us: unfold_strip(): jnp.where(at_top, back_north.astype(jnp.float32), 0.0)]
    add x2 -> x1, other arithmetic: 41 us -> 2.47 us  [unfold_strip(): interior.at[:, :, 0, :]]
    slice x3, local copies, waits for them, and re-layouts: 38.1 us -> 1.21 us  [the longest x1 1.19 us: unfold_strip(): west_part = pad_grad[:, :, 1:-1, 0]]
  transfers between devices with their start and end apart: 17 -> 17, of which waited for: 11 -> 12; matrix products, arithmetic and copies ran while one was open for 13% -> 15% of each run, Pallas kernels for 0% -> 0%
where the time goes in v1:
time: 1360 us; the launch traced here: 1340 us
  local copies, waits for them, and re-layouts  497 us (37%)
  waiting for transfers between devices  421 us (31%)
  matrix products  184 us (14%)
  other arithmetic  165 us (12%)
  blocking collectives  39.3 us (3%)
  starting transfers between devices  21.8 us (2%)
  between operations  15.7 us (1%)
    conv_general_dilated x17, local copies, waits for them, and re-layouts, convolve(): lax.conv_general_dilated(padded, weight, (1, 1), 'VALID', dimension_numbe...  240 us
    all_gather x4, waiting for transfers between devices, partner_pieces(): gathered = lax.all_gather(front, ('face', 'tile'), axis=3, tiled=True)  186 us
    all_gather x4, waiting for transfers between devices, place_lines(): own_lines = lax.all_gather(placed.astype(jnp.bfloat16), 'tile').sum(axis=0)  169 us
    conv_general_dilated x2, matrix products, weight_grad(): lax.conv_general_dilated(padded, cotangent, (1, 1), 'VALID', dimension_nu...  94.3 us
    conv_general_dilated x4, matrix products, convolve(): lax.conv_general_dilated(padded, weight, (1, 1), 'VALID', dimension_numbe...  89.9 us
    unnamed x135, local copies, waits for them, and re-layouts  89.3 us
    conv_general_dilated x4, other arithmetic, convolve(): lax.conv_general_dilated(padded, weight, (1, 1), 'VALID', dimension_numbe...  59.8 us
    add x4, local copies, waits for them, and re-layouts, gelu_pair(): return (values * normal_cdf, normal_cdf + values * normal_pdf)  45.1 us
  transfers between devices with their start and end apart: 17, of which 12 were waited for; matrix products, arithmetic and copies ran while one was open for 15% of the time, Pallas kernels for 0%

profile of v1, /device:TPU:0, one launch (start us, length us, event | category | flops | bytes accessed | tf_op | source)
XLA Modules:
  0.0 1343.4 jit_solution(3858315737199617512)
XLA Ops:
  18.4 55.7 %all-gather.9.cloned.1.call-done = bf16[8,3,4,48,256]{4,3,2,1,0:T(8,128)(2,1)} async-done(((bf16[1,3,4,48,256]{4,3,2,1,0:T(8,128)(2,1)}), bf16[8,3,4,48,256]{4,3,2,1,0:T(8,128)(2,1)}) %all-gather.9.cloned.1.call-update) | async-done | bytes 2359312 | tf_op jit(solution)/shard_map/all_gather | solution.py:59
  85.5 49.8 %all-gather.11.cloned.1.call-done = bf16[3,4,48,1024]{2,1,0,3:T(4,128)(2,1)} async-done(((bf16[3,4,48,32]{2,1,0,3:T(4,128)(2,1)}), bf16[3,4,48,1024]{2,1,0,3:T(4,128)(2,1)}) %all-gather.11.cloned.1.call-update) | async-done | bytes 1179664 | tf_op jit(solution)/shard_map/all_gather | solution.py:71
  158.8 17.8 %fusion.98 = bf16[48,34,3,258]{0,2,3,1:T(4,128)(2,1)S(1)} fusion(bf16[3,48,1,258]{1,0,3,2:T(4,128)(2,1)S(1)} %maximum_select_fusion.1, bf16[3,48,32,1]{1,0,3,2:T(4,128)(2,1)S(1)} %copy.687, bf16[3,48,32,256]{1,0,3,2:T(4,128)(2,1)S(1)} %copy-done.2, bf16[3,48,32,1]{1,0,3,2:T(4,128)(2,1)S(1)} %copy.685, bf16[3,48,1,258]{1,0,3,2:T(4,128)(2,1)S(1)} %maximum_select_fusion), kind=kLoop, calls=%fused_computation.249 | loop fusion | flops 5052672 | bytes 5052672 | tf_op jit(solution)/shard_map/concatenate | solution.py:112
  183.2 24.2 %copy.775 = bf16[48,34,3,8,33]{4,3,0,2,1:T(8,128)(2,1)} copy(bf16[48,34,3,8,33]{0,2,4,3,1:T(4,128)(2,1)} %bitcast.312) | data formatting | bytes 5170176 | tf_op jit(solution)/shard_map/conv_general_dilated | solution.py:34
  219.1 14.9 %fusion.14 = bf16[48,34,3,8,35]{4,3,0,2,1:T(8,128)(2,1)} fusion(bf16[48,34,3,7,2]{4,3,0,2,1:T(8,128)(2,1)} %slice.977, bf16[48,34,3,8,33]{4,3,0,2,1:T(8,128)(2,1)} %copy.775), kind=kLoop, calls=%fused_computation.31 | loop fusion | flops 8225280 | bytes 5463936 | tf_op jit(solution)/shard_map/conv_general_dilated | solution.py:34
  234.1 14.1 %copy.690 = bf16[48,34,3,8,35]{0,3,2,4,1:T(8,128)(2,1)} copy(bf16[48,34,3,8,35]{4,3,0,2,1:T(8,128)(2,1)} %fusion.14) | data formatting | bytes 5483520 | tf_op jit(solution)/shard_map/conv_general_dilated | solution.py:34
  248.2 23.5 %fusion.7 = (f32[32,24,33,48]{3,1,2,0:T(8,128)}, bf16[32,24,33,48]{3,1,2,0:T(8,128)(2,1)S(1)}) fusion(f32[48]{0:T(128)S(1)} %copy-done.51, pred[24,33]{0,1:T(8,128)(4,1)S(1)} %copy-done.55, bf16[48,48,3,3]{1,0,3,2:T(8,128)(2,1)S(1)} %copy-done.49, bf16[48,34,3,8,35]{0,3,2,4,1:T(8,128)(2,1)} %copy.690), kind=kOutput, calls=%fused_computation.16 | convolution fusion | flops 1065664512 | bytes 10083288 | tf_op jit(solution)/shard_map/conv_general_dilated | solution.py:34
  291.2 53.6 %all-gather.13.cloned.1.call-done = bf16[8,3,4,48,256]{4,3,2,1,0:T(8,128)(2,1)} async-done(((bf16[1,3,4,48,256]{4,3,2,1,0:T(8,128)(2,1)}), bf16[8,3,4,48,256]{4,3,2,1,0:T(8,128)(2,1)}) %all-gather.13.cloned.1.call-update) | async-done | bytes 2359312 | tf_op jit(solution)/shard_map/all_gather | solution.py:59
  348.2 57.5 %all-gather.15.cloned.1.call-done = bf16[3,4,48,1024]{2,1,0,3:T(4,128)(2,1)} async-done(((bf16[3,4,48,32]{2,1,0,3:T(4,128)(2,1)}), bf16[3,4,48,1024]{2,1,0,3:T(4,128)(2,1)}) %all-gather.15.cloned.1.call-update) | async-done | bytes 1179664 | tf_op jit(solution)/shard_map/all_gather | solution.py:71
  428.9 19.1 %fusion.95 = bf16[48,34,3,258]{0,2,3,1:T(4,128)(2,1)S(1)} fusion(bf16[3,48,1,258]{1,0,3,2:T(4,128)(2,1)S(1)} %maximum_select_fusion.3, bf16[3,48,32,1]{1,0,3,2:T(4,128)(2,1)S(1)} %copy.708, bf16[3,48,32,256]{1,0,3,2:T(4,128)(2,1)} %bitcast.307, bf16[3,48,32,1]{1,0,3,2:T(4,128)(2,1)S(1)} %copy.707, bf16[3,48,1,258]{1,0,3,2:T(4,128)(2,1)S(1)} %maximum_select_fusion.2), kind=kLoop, calls=%fused_computation.246 | loop fusion | flops 5052672 | bytes 5052672 | tf_op jit(solution)/shard_map/concatenate | solution.py:112
  454.7 24.2 %copy.780 = bf16[48,34,3,8,33]{4,3,0,2,1:T(8,128)(2,1)} copy(bf16[48,34,3,8,33]{0,2,4,3,1:T(4,128)(2,1)} %bitcast.313) | data formatting | bytes 5170176 | tf_op jit(solution)/shard_map/conv_general_dilated | solution.py:34
  490.6 14.9 %fusion.15 = bf16[48,34,3,8,35]{4,3,0,2,1:T(8,128)(2,1)} fusion(bf16[48,34,3,7,2]{4,3,0,2,1:T(8,128)(2,1)} %slice.997, bf16[48,34,3,8,33]{4,3,0,2,1:T(8,128)(2,1)} %copy.780), kind=kLoop, calls=%fused_computation.32 | loop fusion | flops 8225280 | bytes 5463936 | tf_op jit(solution)/shard_map/conv_general_dilated | solution.py:34
  505.5 14.0 %copy.711 = bf16[48,34,3,8,35]{0,3,2,4,1:T(8,128)(2,1)} copy(bf16[48,34,3,8,35]{4,3,0,2,1:T(8,128)(2,1)} %fusion.15) | data formatting | bytes 5483520 | tf_op jit(solution)/shard_map/conv_general_dilated | solution.py:34
  519.5 22.3 %fusion.11 = (f32[32,24,33,48]{3,1,2,0:T(8,128)}, bf16[32,24,33,48]{3,1,2,0:T(8,128)(2,1)}) fusion(f32[48]{0:T(128)S(1)} %copy-done.52, pred[24,33]{0,1:T(8,128)(4,1)S(1)} %copy-done.55, bf16[48,48,3,3]{1,0,3,2:T(8,128)(2,1)S(1)} %copy-done, bf16[48,34,3,8,35]{0,3,2,4,1:T(8,128)(2,1)} %copy.711), kind=kOutput, calls=%fused_computation.20 | convolution fusion | flops 1065664512 | bytes 10083288 | tf_op jit(solution)/shard_map/conv_general_dilated | solution.py:34
  600.2 14.1 %reshape.2059 = bf16[48,34,3,8,33]{4,3,0,2,1:T(8,128)(2,1)} reshape(bf16[48,34,3,264]{3,0,2,1:T(8,128)(2,1)} %pad.64.clone) | data formatting | bytes 5170176 | tf_op jit(solution)/shard_map/conv_general_dilated | solution.py:34
  626.0 14.9 %fusion.16 = bf16[48,34,3,8,35]{4,3,0,2,1:T(8,128)(2,1)} fusion(bf16[48,34,3,7,2]{4,3,0,2,1:T(8,128)(2,1)} %slice.1000, bf16[48,34,3,8,33]{4,3,0,2,1:T(8,128)(2,1)} %reshape.2059), kind=kLoop, calls=%fused_computation.33 | loop fusion | flops 8225280 | bytes 5463936 | tf_op jit(solution)/shard_map/conv_general_dilated | solution.py:34
  641.0 14.0 %copy.719 = bf16[48,34,3,8,35]{0,3,2,4,1:T(8,128)(2,1)} copy(bf16[48,34,3,8,35]{4,3,0,2,1:T(8,128)(2,1)} %fusion.16) | data formatting | bytes 5483520 | tf_op jit(solution)/shard_map/conv_general_dilated | solution.py:34
  655.0 22.2 %convolution_select_fusion.1 = f32[34,24,33,48]{3,1,2,0:T(8,128)} fusion(bf16[48,48,3,3]{1,0,3,2:T(8,128)(2,1)S(1)} %copy-done, bf16[48,34,3,8,35]{0,3,2,4,1:T(8,128)(2,1)} %copy.719, pred[24,33]{0,1:T(8,128)(4,1)S(1)} %copy-done.53), kind=kOutput, calls=%fused_computation.36 | convolution fusion | flops 1096153344 | bytes 7954200 | tf_op jit(solution)/shard_map/conv_general_dilated | solution.py:34
  690.7 15.8 %reshape.2063 = f32[34,3,264,48]{3,2,1,0:T(8,128)} reshape(f32[34,24,33,48]{3,2,1,0:T(8,128)} %copy.720) | data formatting | bytes 10340352 | tf_op jit(solution)/shard_map/conv_general_dilated | solution.py:34
  724.0 55.0 %all-gather.17.cloned.1.call-done = bf16[8,3,4,48,256]{4,3,2,1,0:T(8,128)(2,1)} async-done(((bf16[1,3,4,48,256]{4,3,2,1,0:T(8,128)(2,1)}), bf16[8,3,4,48,256]{4,3,2,1,0:T(8,128)(2,1)}) %all-gather.17.cloned.1.call-update) | async-done | bytes 2359312 | tf_op jit(solution)/shard_map/all_gather | solution.py:59
  822.9 17.1 %all-gather.19.cloned.1.call-done = bf16[3,4,48,1024]{2,1,0,3:T(4,128)(2,1)} async-done(((bf16[3,4,48,32]{2,1,0,3:T(4,128)(2,1)}), bf16[3,4,48,1024]{2,1,0,3:T(4,128)(2,1)}) %all-gather.19.cloned.1.call-update) | async-done | bytes 1179664 | tf_op jit(solution)/shard_map/all_gather | solution.py:71
  857.0 14.0 %convert_reduce_fusion = (f32[48]{0:T(128)}, bf16[3,48,32,256]{1,3,0,2:T(8,128)(2,1)S(1)}) fusion(f32[3,48,32,256]{1,3,0,2:T(8,128)} %scatter-add.99, f32[32,3,256,48]{3,0,2,1:T(8,128)} %slice.1027), kind=kLoop, calls=%fused_computation.30 | loop fusion | flops 4718544 | bytes 11796672 | tf_op jit(solution)/shard_map/reduce_sum | solution.py:215
  879.9 45.5 %fusion.87 = f32[48,48,3,3]{0,1,3,2:T(8,128)} fusion(bf16[3,48,32,256]{1,0,3,2:T(4,128)(2,1)} %copy.766, bf16[3,48,1,258]{1,0,3,2:T(4,128)(2,1)S(1)} %copy-done.17, bf16[3,48,32,1]{1,0,3,2:T(4,128)(2,1)S(1)} %copy-done.23, bf16[3,48,32,256]{1,0,3,2:T(4,128)(2,1)} %bitcast.308, bf16[3,48,32,1]{1,0,3,2:T(4,128)(2,1)S(1)} %copy-done.25, ...), kind=kOutput, calls=%fused_computation.245 | convolution fusion | flops 1031847552 | bytes 4968576 | tf_op jit(solution)/shard_map/conv_general_dilated | solution.py:172
  946.8 14.1 %reshape.2066 = bf16[48,34,3,8,33]{4,3,0,2,1:T(8,128)(2,1)} reshape(bf16[48,34,3,264]{3,0,2,1:T(8,128)(2,1)} %pad.66.clone) | data formatting | bytes 5170176 | tf_op jit(solution)/shard_map/conv_general_dilated | solution.py:34
  972.7 14.9 %fusion.17 = bf16[48,34,3,8,35]{4,3,0,2,1:T(8,128)(2,1)} fusion(bf16[48,34,3,7,2]{4,3,0,2,1:T(8,128)(2,1)} %slice.1028, bf16[48,34,3,8,33]{4,3,0,2,1:T(8,128)(2,1)} %reshape.2066), kind=kLoop, calls=%fused_computation.34 | loop fusion | flops 8225280 | bytes 5463936 | tf_op jit(solution)/shard_map/conv_general_dilated | solution.py:34
  987.6 14.1 %copy.747 = bf16[48,34,3,8,35]{0,3,2,4,1:T(8,128)(2,1)} copy(bf16[48,34,3,8,35]{4,3,0,2,1:T(8,128)(2,1)} %fusion.17) | data formatting | bytes 5483520 | tf_op jit(solution)/shard_map/conv_general_dilated | solution.py:34
  1001.7 22.0 %convolution_select_fusion = f32[34,24,33,48]{3,1,2,0:T(8,128)} fusion(bf16[48,48,3,3]{1,0,3,2:T(8,128)(2,1)S(1)} %copy-done.50, bf16[48,34,3,8,35]{0,3,2,4,1:T(8,128)(2,1)} %copy.747, pred[24,33]{0,1:T(8,128)(4,1)S(1)} %copy-done.54), kind=kOutput, calls=%fused_computation.35 | convolution fusion | flops 1096153344 | bytes 7954200 | tf_op jit(solution)/shard_map/conv_general_dilated | solution.py:34
  1054.1 48.8 %fusion.18 = f32[48,48,3,3]{0,1,3,2:T(8,128)} fusion(bf16[3,48,32,256]{1,3,0,2:T(8,128)(2,1)} %copy-done.3, bf16[3,48,1,258]{1,0,3,2:T(4,128)(2,1)S(1)} %copy-done.13, bf16[3,48,32,1]{1,0,3,2:T(4,128)(2,1)S(1)} %copy-done.19, bf16[3,48,32,256]{1,0,3,2:T(4,128)(2,1)} %copy.686, bf16[3,48,32,1]{1,0,3,2:T(4,128)(2,1)S(1)} %copy-done.21, ...), kind=kOutput, calls=%fused_computation.40 | convolution fusion | flops 1031847552 | bytes 4968576 | tf_op jit(solution)/shard_map/conv_general_dilated | solution.py:172
  1128.2 39.3 %all-reduce.2 = (f32[48]{0:T(128)S(1)}, f32[48]{0:T(128)S(1)}) all-reduce(f32[48]{0:T(128)S(1)} %copy-done.48, f32[48]{0:T(128)S(1)} %copy-done.47), channel_id=1, replica_groups=mesh['face'=4,'tile'=8] {'face','tile'}, use_global_device_ids=true, to_apply=%region_6.7 | all-reduce | flops 96 | bytes 768 | tf_op jit(solution)/shard_map/psum | solution.py:219
  1180.0 16.4 %copy.814 = f32[3,48,32,256]{1,3,0,2:T(8,128)} copy(f32[3,48,32,256]{1,2,3,0:T(8,128)} %slice.1030) | data formatting | bytes 9437184
  1196.4 41.8 %all-reduce.6.cloned.1.call-done = (f32[48,48,3,3]{0,1,3,2:T(8,128)}, f32[48,48,3,3]{0,1,3,2:T(8,128)}) async-done(((f32[48,48,3,3]{0,1,3,2:T(8,128)}, f32[48,48,3,3]{0,1,3,2:T(8,128)}), (f32[48,48,3,3]{0,1,3,2:T(8,128)}, f32[48,48,3,3]{0,1,3,2:T(8,128)})) %all-reduce.6.cloned.1.call-update) | async-done | bytes 165904 | tf_op jit(solution)/shard_map/psum | solution.py:219
  1240.9 61.3 %all-gather.23.cloned.1.call-done = bf16[3,4,48,1024]{2,1,0,3:T(4,128)(2,1)} async-done(((bf16[3,4,48,32]{2,1,0,3:T(4,128)(2,1)}), bf16[3,4,48,1024]{2,1,0,3:T(4,128)(2,1)}) %all-gather.23.cloned.1.call-update) | async-done | bytes 1179664 | tf_op jit(solution)/shard_map/all_gather | solution.py:71
  (372 shorter events, 436.7 us)
Async XLA Ops:
  7.2 512.3 %copy-start = (bf16[48,48,3,3]{1,0,3,2:T(8,128)(2,1)S(1)}, bf16[48,48,3,3]{1,0,3,2:T(8,128)(2,1)}, u32[]{:S(2)}) copy-start(bf16[48,48,3,3]{1,0,3,2:T(8,128)(2,1)} %param.60) | copy-start | bytes 124420
  7.2 66.9 %all-gather.9.cloned.1.call-start = ((), (), s32[]{:S(2)}) async-start(), calls=%async_computation | async-start | bytes 2654208 | tf_op jit(solution)/shard_map/all_gather | solution.py:59
  12.5 71.4 %copy-start.26 = (s32[12,4,3]{0,1,2:T(4,128)S(1)}, s32[12,4,3]{0,1,2:T(4,128)}, u32[]{:S(2)}) copy-start(s32[12,4,3]{0,1,2:T(4,128)} %param.62) | copy-start | bytes 1732
  12.5 71.9 %copy-start.46 = (s32[12,4]{0,1:T(4,128)S(1)}, s32[12,4]{0,1:T(4,128)}, u32[]{:S(2)}) copy-start(s32[12,4]{0,1:T(4,128)} %param.63) | copy-start | bytes 580
  18.3 116.9 %all-gather.11.cloned.1.call-start = ((), (), s32[]{:S(2)}) async-start(), calls=%async_computation.1 | async-start | bytes 3244032 | tf_op jit(solution)/shard_map/all_gather | solution.py:71
  77.0 267.7 %all-gather.13.cloned.1.call-start = ((), (), s32[]{:S(2)}) async-start(), calls=%async_computation.2 | async-start | bytes 2654208 | tf_op jit(solution)/shard_map/all_gather | solution.py:59
  84.2 325.4 %copy-start.27 = (pred[12]{0:T(512)(128)(4,1)}, pred[12]{0:T(512)(128)(4,1)S(1)}, u32[]{:S(2)}) copy-start(pred[12]{0:T(512)(128)(4,1)S(1)} %eq.133) | copy-start | bytes 40
  85.4 320.3 %copy-start.7 = (s32[12]{0:T(128)}, s32[12]{0:T(128)S(1)}, u32[]{:S(2)}) copy-start(s32[12]{0:T(128)S(1)} %fusion.73) | copy-start | bytes 148
  143.0 15.3 %collective-permute-start = (bf16[3,48,1,258]{1,0,3,2:T(4,128)(2,1)S(1)}, bf16[3,48,1,258]{1,0,3,2:T(4,128)(2,1)S(1)}, u32[]{:S(2)}, u32[]{:S(2)}) collective-permute-start(bf16[3,48,1,258]{1,0,3,2:T(4,128)(2,1)S(1)} %get-tuple-element.393), channel_id=1, source_target_pairs={{0,1},{1,2},{2,3},{3,4},{4,5},{5,6},{6,7},{8,9},{9,10},{10,11},{11... | collective-permute-start | bytes 222920 | tf_op jit(solution)/shard_map/ppermute | solution.py:19
  146.6 11.9 collective-permute-start.1
  291.1 114.6 %all-gather.15.cloned.1.call-start = ((), (), s32[]{:S(2)}) async-start(), calls=%async_computation.3 | async-start | bytes 3244032 | tf_op jit(solution)/shard_map/all_gather | solution.py:71
  347.7 431.3 %all-gather.17.cloned.1.call-start = ((), (), s32[]{:S(2)}) async-start(), calls=%async_computation.4 | async-start | bytes 2654208 | tf_op jit(solution)/shard_map/all_gather | solution.py:59
  413.3 15.0 %collective-permute-start.2 = (bf16[3,48,1,258]{1,0,3,2:T(4,128)(2,1)S(1)}, bf16[3,48,1,258]{1,0,3,2:T(4,128)(2,1)S(1)}, u32[]{:S(2)}, u32[]{:S(2)}) collective-permute-start(bf16[3,48,1,258]{1,0,3,2:T(4,128)(2,1)S(1)} %get-tuple-element.391), channel_id=1, source_target_pairs={{0,1},{1,2},{2,3},{3,4},{4,5},{5,6},{6,7},{8,9},{9,10},{10,11},{11... | collective-permute-start | bytes 222920 | tf_op jit(solution)/shard_map/ppermute | solution.py:19
  416.7 11.9 collective-permute-start.3
  581.5 13.4 collective-permute-start.4
  586.0 9.0 collective-permute-start.5
  587.6 132.2 %copy-start.34 = (pred[3]{0:T(512)(128)(4,1)}, pred[3]{0:T(512)(128)(4,1)S(1)}, u32[]{:S(2)}) copy-start(pred[3]{0:T(512)(128)(4,1)S(1)} %get-tuple-element.343) | copy-start | bytes 13
  587.6 132.2 %copy-start.40 = (pred[3]{0:T(512)(128)(4,1)}, pred[3]{0:T(512)(128)(4,1)S(1)}, u32[]{:S(2)}) copy-start(pred[3]{0:T(512)(128)(4,1)S(1)} %get-tuple-element.344) | copy-start | bytes 13
  587.6 132.2 %copy-start.42 = (pred[3]{0:T(512)(128)(4,1)}, pred[3]{0:T(512)(128)(4,1)S(1)}, u32[]{:S(2)}) copy-start(pred[3]{0:T(512)(128)(4,1)S(1)} %get-tuple-element.348) | copy-start | bytes 13
  587.6 132.2 %copy-start.44 = (pred[3]{0:T(512)(128)(4,1)}, pred[3]{0:T(512)(128)(4,1)S(1)}, u32[]{:S(2)}) copy-start(pred[3]{0:T(512)(128)(4,1)S(1)} %get-tuple-element.349) | copy-start | bytes 13
  587.6 133.3 %copy-start.30 = (pred[3]{0:T(512)(128)(4,1)}, pred[3]{0:T(512)(128)(4,1)S(1)}, u32[]{:S(2)}) copy-start(pred[3]{0:T(512)(128)(4,1)S(1)} %get-tuple-element.345) | copy-start | bytes 13
  587.6 133.3 %copy-start.32 = (pred[3]{0:T(512)(128)(4,1)}, pred[3]{0:T(512)(128)(4,1)S(1)}, u32[]{:S(2)}) copy-start(pred[3]{0:T(512)(128)(4,1)S(1)} %get-tuple-element.342) | copy-start | bytes 13
  587.6 133.3 %copy-start.36 = (pred[3]{0:T(512)(128)(4,1)}, pred[3]{0:T(512)(128)(4,1)S(1)}, u32[]{:S(2)}) copy-start(pred[3]{0:T(512)(128)(4,1)S(1)} %get-tuple-element.346) | copy-start | bytes 13
  587.6 133.3 %copy-start.38 = (pred[3]{0:T(512)(128)(4,1)}, pred[3]{0:T(512)(128)(4,1)S(1)}, u32[]{:S(2)}) copy-start(pred[3]{0:T(512)(128)(4,1)S(1)} %get-tuple-element.347) | copy-start | bytes 13
  723.9 116.1 %all-gather.19.cloned.1.call-start = ((), (), s32[]{:S(2)}) async-start(), calls=%async_computation.5 | async-start | bytes 3244032 | tf_op jit(solution)/shard_map/all_gather | solution.py:71
  781.9 325.5 %all-gather.21.cloned.1.call-start = ((), (), s32[]{:S(2)}) async-start(), calls=%async_computation.6 | async-start | bytes 2654208 | tf_op jit(solution)/shard_map/all_gather | solution.py:59
  874.6 53.3 %collective-permute-start.6 = (bf16[3,48,1,258]{1,3,0,2:T(8,128)(2,1)}, bf16[3,48,1,258]{1,3,0,2:T(8,128)(2,1)}, u32[]{:S(2)}, u32[]{:S(2)}) collective-permute-start(bf16[3,48,1,258]{1,3,0,2:T(8,128)(2,1)} %get-tuple-element.397), channel_id=1, source_target_pairs={{0,1},{1,2},{2,3},{3,4},{4,5},{5,6},{6,7},{8,9},{9,10},{10,11},{11... | collective-permute-start | bytes 222920 | tf_op jit(solution)/shard_map/ppermute | solution.py:19
  878.6 49.3 %collective-permute-start.7 = (bf16[3,48,1,258]{1,3,0,2:T(8,128)(2,1)}, bf16[3,48,1,258]{1,3,0,2:T(8,128)(2,1)}, u32[]{:S(2)}, u32[]{:S(2)}) collective-permute-start(bf16[3,48,1,258]{1,3,0,2:T(8,128)(2,1)} %get-tuple-element.398), channel_id=1, source_target_pairs={{1,0},{2,1},{3,2},{4,3},{5,4},{6,5},{7,6},{9,8},{10,9},{11,10},{12... | collective-permute-start | bytes 222920 | tf_op jit(solution)/shard_map/ppermute | solution.py:22
  1054.0 184.1 %all-reduce.6.cloned.1.call-start = ((), (), s32[]{:S(2)}) async-start(), calls=%async_computation.8 | async-start | bytes 884736 | tf_op jit(solution)/shard_map/psum | solution.py:219
  1102.9 199.3 %all-gather.23.cloned.1.call-start = ((), (), s32[]{:S(2)}) async-start(), calls=%async_computation.7 | async-start | bytes 3244032 | tf_op jit(solution)/shard_map/all_gather | solution.py:71
  1180.0 122.2 %copy-start.9 = (s32[12]{0:T(128)S(1)}, s32[12]{0:T(128)}, u32[]{:S(2)}) copy-start(s32[12]{0:T(128)} %copy-done.7) | copy-start | bytes 148
  1180.0 126.2 %copy-start.29 = (pred[12]{0:T(512)(128)(4,1)S(1)}, pred[12]{0:T(512)(128)(4,1)}, u32[]{:S(2)}) copy-start(pred[12]{0:T(512)(128)(4,1)} %copy-done.27) | copy-start | bytes 40
  (41 other events, 838.4 us)
Sparse Core Ops, SparseCore 0:
  18.4 55.6 all-gather.8
  77.6 57.6 all-gather.10
  291.2 53.4 all-gather.12
  348.1 57.6 all-gather.14
  724.0 54.9 all-gather.16
  782.3 57.6 all-gather.18
  1054.2 53.1 all-gather.20
  1113.3 124.8 all-reduce.5
  1242.1 60.0 all-gather.22
